TPU v7x, 128 devices: a whole 4x4x4 slice. The times are simulated.
128 devices in a mesh: row: 8 (over x, z_lo), col: 16 (over y, z_hi, core).
Axes of the slice: x: 4, y: 4, z: 4 (z_hi: 2, z_lo: 2; z = z_hi * 2 + z_lo), core: 2. Of those that a mesh axis runs over, the one named last changes fastest.
Arguments:
- tokens_in: bfloat16 [8192, 5120], P('row', 'col'), may hold values from -6 to 6
- token_grad: bfloat16 [8192, 5120], P('row', 'col'), may hold values from -6 to 6
- gate_gain: float32 [5120], replicated, may hold values from -4 to 4
- inner_weight: bfloat16 [5120, 13824], P(None, 'col'), may hold values from -0.078125 to 0.078125
- inner_bias: float32 [13824], P('col'), may hold values from -4 to 4
- outer_weight: bfloat16 [5120, 13824], P(None, 'col'), may hold values from -0.0546875 to 0.0546875
- inner_down: bfloat16 [5120, 64], replicated, may hold values from -0.078125 to 0.078125
- inner_up: bfloat16 [64, 13824], P(None, 'col'), may hold values from -0.1796875 to 0.1796875
- outer_down: bfloat16 [13824, 64], P('col'), may hold values from -0.0546875 to 0.0546875
- outer_up: bfloat16 [64, 5120], replicated, may hold values from -0.1796875 to 0.1796875
Outputs:
- tokens_grad: bfloat16 [8192, 5120], P('row', 'col')
- inner_down_grad: float32 [5120, 64], P('col')
- inner_up_grad: float32 [64, 13824], P(None, 'col')
- outer_down_grad: float32 [13824, 64], P('col')
- outer_up_grad: float32 [64, 5120], P(None, 'col')
All inputs are finite; a program needn't handle non-finite values.
Results may differ from a plain program's by a relative error of at most 0.023.
Values may be sent and summed in bfloat16 or wider, within the bound.
A program may use at most 128 MiB of HBM per device.

v0:
```python
import math
import jax
import jax.numpy as jnp
from jax import lax
from jax.sharding import PartitionSpec as P

SLOPE_SCALE = 0.7978845608028654
CUBIC = 0.044715


def gelu_value(pre):
    inner = SLOPE_SCALE * (pre + CUBIC * pre * pre * pre)
    return 0.5 * pre * (1.0 + jnp.tanh(inner))


def gelu_slope(pre):
    tangent = jnp.tanh(SLOPE_SCALE * (pre + CUBIC * pre * pre * pre))
    return 0.5 * (1.0 + tangent) + 0.5 * pre * (1.0 - tangent * tangent) * SLOPE_SCALE * (
        1.0 + 3.0 * CUBIC * pre * pre
    )


def plain_dot(left, right):
    return jnp.dot(left, right, preferred_element_type=jnp.float32)


def dot_rows(left, right):
    return lax.dot_general(
        left, right, (((1,), (1,)), ((), ())), preferred_element_type=jnp.float32
    )


def dot_cols(left, right):
    return lax.dot_general(
        left, right, (((0,), (0,)), ((), ())), preferred_element_type=jnp.float32
    )


def tree_sum(value, axis, size):
    step = 1
    while step < size:
        pairs = [(i, i ^ step) for i in range(size)]
        value = value + lax.ppermute(value, axis, pairs)
        step *= 2
    return value


def local(
    tokens_in,
    token_grad,
    gate_gain,
    inner_weight,
    inner_bias,
    outer_weight,
    inner_down,
    inner_up,
    outer_down,
    outer_up,
):
    n_col = lax.axis_size("col")
    n_row = lax.axis_size("row")
    col_index = lax.axis_index("col")
    local_width = token_grad.shape[1]
    tok_rows = tokens_in.shape[0]
    ff_local = inner_weight.shape[1]
    rank = inner_down.shape[1]
    gain_local = lax.dynamic_slice_in_dim(gate_gain, col_index * local_width, local_width, 0)
    gated_local = (gain_local[None, :] * token_grad.astype(jnp.float32)).astype(jnp.bfloat16)
    both_full = lax.all_gather(jnp.stack([tokens_in, gated_local]), "col", axis=2, tiled=True)
    tokens_full, gated_full = (both_full[0], both_full[1])
    inner_cat = jnp.concatenate([inner_weight, inner_down], axis=1)
    outer_cat = jnp.concatenate([outer_weight, outer_up.T], axis=1)
    forward_all = plain_dot(tokens_full, inner_cat)
    forward_sum = forward_all[:, :ff_local]
    inner_low = forward_all[:, ff_local:].astype(jnp.bfloat16)
    backward_all = plain_dot(gated_full, outer_cat)
    backward_sum = backward_all[:, :ff_local]
    grad_low = backward_all[:, ff_local:].astype(jnp.bfloat16)
    pre = forward_sum + plain_dot(inner_low, inner_up) + inner_bias[None, :]
    hidden = gelu_value(pre).astype(jnp.bfloat16)
    grad_hidden = backward_sum + dot_rows(grad_low, outer_down)
    grad_pre = (grad_hidden * gelu_slope(pre)).astype(jnp.bfloat16)
    pre_low_part = dot_rows(grad_pre, inner_up)
    block_part = dot_rows(grad_pre, inner_weight).astype(jnp.bfloat16).astype(jnp.float32)
    low_part = dot_rows(pre_low_part.astype(jnp.bfloat16), inner_down)
    tokens_grad = lax.psum_scatter(
        (block_part + low_part).astype(jnp.bfloat16), "col", scatter_dimension=1, tiled=True
    )
    hidden_low_part = plain_dot(hidden, outer_down)
    lows = tree_sum(jnp.concatenate([hidden_low_part, pre_low_part], axis=1), "col", n_col)
    hidden_low = lows[:, :rank].astype(jnp.bfloat16)
    pre_low = lows[:, rank:].astype(jnp.bfloat16)
    scale = 1.0 / math.sqrt(tok_rows * n_row)
    outer_down_term = dot_cols(hidden, grad_low)
    outer_up_term = dot_cols(gated_local, hidden_low)
    inner_down_term = dot_cols(tokens_in, pre_low)
    inner_up_term = dot_cols(grad_pre, inner_low)
    packed = jnp.concatenate(
        [outer_down_term, inner_up_term, outer_up_term, inner_down_term], axis=0
    )
    packed = tree_sum(packed, "row", n_row) * scale
    outer_down_grad = packed[:ff_local]
    inner_up_grad = packed[ff_local : 2 * ff_local].T
    outer_up_grad = packed[2 * ff_local : 2 * ff_local + local_width].T
    inner_down_grad = packed[2 * ff_local + local_width :]
    return (tokens_grad, inner_down_grad, inner_up_grad, outer_down_grad, outer_up_grad)


def solution(mesh):
    placed = (
        P("row", "col"),
        P("row", "col"),
        P(),
        P(None, "col"),
        P("col"),
        P(None, "col"),
        P(),
        P(None, "col"),
        P("col", None),
        P(),
    )
    return jax.shard_map(
        local,
        mesh=mesh,
        in_specs=placed,
        out_specs=(P("row", "col"), P("col", None), P(None, "col"), P("col", None), P(None, "col")),
        check_vma=False,
    )
```

profile of v0, /device:TPU:1, one launch (start us, length us, event | category | flops | bytes accessed | tf_op | source)
XLA Modules:
  0.0 329.9 jit_solution(954291616641102913)
XLA Ops:
  7.2 0.0 copy-start
  7.2 0.0 copy-start.3
  7.2 0.0 all-gather.2.cloned.1.call-start
  7.2 0.8 dynamic_slice.3
  8.1 1.3 fusion.17
  9.4 2.3 pad_maximum_fusion
  11.7 0.0 all-gather.2.cloned.1.call-update
  11.7 0.0 copy-start.9
  11.7 0.0 reduce-scatter.2.cloned.1.call-start
  11.7 133.4 %all-gather.2.cloned.1.call-done = bf16[2,1024,5120]{1,2,0:T(8,128)(2,1)} async-done(((bf16[2,1024,320]{1,2,0:T(8,128)(2,1)}), bf16[2,1024,5120]{1,2,0:T(8,128)(2,1)}) %all-gather.2.cloned.1.call-update) | async-done | bytes 20971536 | tf_op jit(solution)/shard_map/all_gather | solution.py:69
  145.2 0.0 copy-done.3
  145.2 15.8 %fusion = f32[1024,928]{0,1:T(8,128)S(1)} fusion(bf16[2,1024,5120]{1,2,0:T(8,128)(2,1)} %all-gather.2.cloned.1.call-done, bf16[5120,64]{0,1:T(8,128)(2,1)S(1)} %copy-done.3, bf16[5120,864]{0,1:T(8,128)(2,1)} %param.13), kind=kOutput, calls=%fused_computation.2 | convolution fusion | flops 9749790720 | bytes 23789568 | tf_op jit(solution)/shard_map/dot_general | solution.py:24
  161.0 0.0 copy-done
  161.0 0.0 copy-done.9
  161.0 0.0 copy-start.6
  161.0 0.0 copy-start.8
  161.0 4.0 %multiply_convert_fusion = (bf16[1024,864]{0,1:T(8,128)(2,1)}, f32[1024,864]{0,1:T(8,128)}) fusion(f32[864]{0:T(1024)S(1)} %copy-done.9, bf16[64,864]{1,0:T(8,128)(2,1)S(1)} %copy-done, f32[1024,928]{0,1:T(8,128)S(1)} %fusion), kind=kOutput, calls=%fused_computation.23 | convolution fusion | flops 123043840 | bytes 9223552 | tf_op jit(solution)/shard_map/dot_general | solution.py:24
  165.0 0.0 copy-done.6
  165.0 0.0 copy-done.8
  165.0 15.9 %fusion.1 = f32[1024,928]{0,1:T(8,128)S(1)} fusion(bf16[2,1024,5120]{1,2,0:T(8,128)(2,1)} %all-gather.2.cloned.1.call-done, bf16[5120,64]{0,1:T(8,128)(2,1)S(1)} %bitcast.29, bf16[5120,864]{0,1:T(8,128)(2,1)} %param.15), kind=kOutput, calls=%fused_computation.4 | convolution fusion | flops 9749790720 | bytes 23789568 | tf_op jit(solution)/shard_map/dot_general | solution.py:24
  180.9 0.0 copy-start.7
  180.9 0.0 copy-done.5
  180.9 5.5 %fusion.14 = bf16[1024,864]{0,1:T(8,128)(2,1)S(1)} fusion(f32[1024,864]{0,1:T(8,128)} %get-tuple-element.10, f32[1024,928]{0,1:T(8,128)S(1)} %fusion.1, bf16[864,64]{0,1:T(8,128)(2,1)S(1)} %copy-done.5), kind=kOutput, calls=%fused_computation.19 | convolution fusion | flops 131006464 | bytes 9220096 | tf_op jit(solution)/shard_map/dot_general | solution.py:28
  186.4 0.0 copy-done.7
  186.4 0.4 fusion.28
  186.9 13.7 %fusion.27 = bf16[1024,5120]{0,1:T(8,128)(2,1)S(1)} fusion(bf16[1024,864]{0,1:T(8,128)(2,1)S(1)} %fusion.14, bf16[5120,864]{0,1:T(8,128)(2,1)} %param.13), kind=kOutput, calls=%fused_computation.45 | convolution fusion | flops 9059696640 | bytes 21102592 | tf_op jit(solution)/shard_map/dot_general | solution.py:28
  200.6 6.8 %add_convert_fusion = bf16[1024,5120]{0,1:T(8,128)(2,1)} fusion(bf16[5120,64]{0,1:T(8,128)(2,1)} %param.16, bf16[1024,5120]{0,1:T(8,128)(2,1)S(1)} %fusion.27, f32[1024,64]{0,1:T(8,128)S(1)} %fusion.28), kind=kOutput, calls=%fused_computation | convolution fusion | flops 686882816 | bytes 21889024 | tf_op jit(solution)/shard_map/dot_general | solution.py:28
  207.4 0.0 reduce-scatter.2.cloned.1.call-update
  207.4 0.0 copy-start.1
  207.4 2.0 fusion.29
  209.5 0.3 collective-permute-start
  209.8 1.7 collective-permute-done
  211.5 0.1 fusion.25
  211.6 0.2 collective-permute-start.1
  211.7 14.7 %collective-permute-done.1 = f32[1024,128]{0,1:T(8,128)S(1)} collective-permute-done((f32[1024,128]{0,1:T(8,128)S(1)}, f32[1024,128]{0,1:T(8,128)S(1)}, u32[]{:S(2)}, u32[]{:S(2)}) %collective-permute-start.1) | collective-permute-done | bytes 524320 | tf_op jit(solution)/shard_map/ppermute | solution.py:43
  226.4 0.1 add.68
  226.5 0.0 copy-start.2
  226.5 0.1 collective-permute-start.2
  226.6 12.3 %collective-permute-done.2 = f32[1024,128]{0,1:T(8,128)S(1)} collective-permute-done((f32[1024,128]{0,1:T(8,128)S(1)}, f32[1024,128]{0,1:T(8,128)S(1)}, u32[]{:S(2)}, u32[]{:S(2)}) %collective-permute-start.2) | collective-permute-done | bytes 524320 | tf_op jit(solution)/shard_map/ppermute | solution.py:43
  238.9 0.1 add.69
  239.0 0.0 copy-start.4
  239.0 1.1 collective-permute-start.3
  240.2 0.0 copy-done.1
  240.2 1.6 fusion.21
  241.8 1.6 fusion.22
  243.4 14.5 %collective-permute-done.3 = f32[1024,128]{0,1:T(8,128)S(1)} collective-permute-done((f32[1024,128]{0,1:T(8,128)S(1)}, f32[1024,128]{0,1:T(8,128)S(1)}, u32[]{:S(2)}, u32[]{:S(2)}) %collective-permute-start.3) | collective-permute-done | bytes 524320 | tf_op jit(solution)/shard_map/ppermute | solution.py:43
  257.8 0.1 add_convert_fusion.1
  257.9 0.0 copy-done.2
  257.9 0.3 convolution_bitcast_fusion
  258.3 0.0 copy-done.4
  258.3 0.4 fusion.16
  258.7 0.2 concatenate.15
  258.9 0.1 collective-permute-start.4
  259.0 9.5 %collective-permute-done.4 = f32[2368,64]{0,1:T(8,128)S(1)} collective-permute-done((f32[2368,64]{0,1:T(8,128)S(1)}, f32[2368,64]{0,1:T(8,128)S(1)}, u32[]{:S(2)}, u32[]{:S(2)}) %collective-permute-start.4) | collective-permute-done | bytes 606240 | tf_op jit(solution)/shard_map/ppermute | solution.py:43
  268.5 0.1 add.71
  268.5 1.3 collective-permute-start.5
  269.8 8.3 %collective-permute-done.5 = f32[2368,64]{0,1:T(8,128)S(1)} collective-permute-done((f32[2368,64]{0,1:T(8,128)S(1)}, f32[2368,64]{0,1:T(8,128)S(1)}, u32[]{:S(2)}, u32[]{:S(2)}) %collective-permute-start.5) | collective-permute-done | bytes 606240 | tf_op jit(solution)/shard_map/ppermute | solution.py:43
  278.1 0.1 add.72
  278.2 2.6 collective-permute-start.6
  280.7 8.5 %collective-permute-done.6 = f32[2368,64]{0,1:T(8,128)S(1)} collective-permute-done((f32[2368,64]{0,1:T(8,128)S(1)}, f32[2368,64]{0,1:T(8,128)S(1)}, u32[]{:S(2)}, u32[]{:S(2)}) %collective-permute-start.6) | collective-permute-done | bytes 606240 | tf_op jit(solution)/shard_map/ppermute | solution.py:43
  289.2 0.1 add_multiply_fusion
  289.3 0.7 slice_bitcast_fusion.5
  290.0 0.8 fusion.26
  290.9 32.3 %reduce-scatter.2.cloned.1.call-done = bf16[1024,320]{0,1:T(8,128)(2,1)} async-done(((bf16[1024,5120]{0,1:T(8,128)(2,1)}), bf16[1024,320]{0,1:T(8,128)(2,1)}) %reduce-scatter.2.cloned.1.call-update) | async-done | bytes 655376 | tf_op jit(solution)/shard_map/reduce_scatter | solution.py:86
  (2 shorter events, 0.0 us)
Async XLA Ops:
  7.2 153.8 %copy-start = (bf16[64,864]{1,0:T(8,128)(2,1)S(1)}, bf16[64,864]{1,0:T(8,128)(2,1)}, u32[]{:S(2)}) copy-start(bf16[64,864]{1,0:T(8,128)(2,1)} %param.17) | copy-start | bytes 331780
  7.2 138.0 %copy-start.3 = (bf16[5120,64]{0,1:T(8,128)(2,1)S(1)}, bf16[5120,64]{0,1:T(8,128)(2,1)}, u32[]{:S(2)}) copy-start(bf16[5120,64]{0,1:T(8,128)(2,1)} %param.16) | copy-start | bytes 1966084
  7.2 138.0 %all-gather.2.cloned.1.call-start = ((), (), s32[]{:S(2)}) async-start(), calls=%async_computation.1 | async-start | bytes 22282240 | tf_op jit(solution)/shard_map/all_gather | solution.py:69
  11.7 149.3 %copy-start.9 = (f32[864]{0:T(1024)S(1)}, f32[864]{0:T(1024)}, u32[]{:S(2)}) copy-start(f32[864]{0:T(1024)} %param.14) | copy-start | bytes 10372
  11.7 311.4 %reduce-scatter.2.cloned.1.call-start = ((), (), s32[]{:S(2)}) async-start(), calls=%async_computation.2 | async-start | bytes 11141120 | tf_op jit(solution)/shard_map/reduce_scatter | solution.py:86
  161.0 4.0 %copy-start.6 = (f32[1024,928]{0,1:T(8,128)}, f32[1024,928]{0,1:T(8,128)S(1)}, u32[]{:S(2)}) copy-start(f32[1024,928]{0,1:T(8,128)S(1)} %fusion) | copy-start | bytes 11403268
  161.0 4.0 %copy-start.8 = (bf16[64,5120]{1,0:T(8,128)(2,1)S(1)}, bf16[64,5120]{1,0:T(8,128)(2,1)}, u32[]{:S(2)}) copy-start(bf16[64,5120]{1,0:T(8,128)(2,1)} %param.19) | copy-start | bytes 1966084
  165.0 15.9 %copy-start.5 = (bf16[864,64]{0,1:T(8,128)(2,1)S(1)}, bf16[864,64]{0,1:T(8,128)(2,1)}, u32[]{:S(2)}) copy-start(bf16[864,64]{0,1:T(8,128)(2,1)} %param.18) | copy-start | bytes 331780
  180.9 5.5 %copy-start.7 = (f32[1024,928]{0,1:T(8,128)}, f32[1024,928]{0,1:T(8,128)S(1)}, u32[]{:S(2)}) copy-start(f32[1024,928]{0,1:T(8,128)S(1)} %fusion.1) | copy-start | bytes 11403268
  207.4 32.8 %copy-start.1 = (bf16[1024,864]{0,1:T(8,128)(2,1)S(1)}, bf16[1024,864]{0,1:T(8,128)(2,1)}, u32[]{:S(2)}) copy-start(bf16[1024,864]{0,1:T(8,128)(2,1)} %get-tuple-element.9) | copy-start | bytes 5308420
  209.5 2.0 collective-permute-start
  211.6 14.9 %collective-permute-start.1 = (f32[1024,128]{0,1:T(8,128)S(1)}, f32[1024,128]{0,1:T(8,128)S(1)}, u32[]{:S(2)}, u32[]{:S(2)}) collective-permute-start(f32[1024,128]{0,1:T(8,128)S(1)} %fusion.25), channel_id=1, source_target_pairs={{0,2},{1,3},{2,0},{3,1},{4,6},{5,7},{6,4},{7,5},{8,10},{9,11},{10,... | collective-permute-start | bytes 1572872 | tf_op jit(solution)/shard_map/ppermute | solution.py:43
  226.5 31.4 %copy-start.2 = (bf16[1024,320]{0,1:T(8,128)(2,1)S(1)}, bf16[1024,320]{0,1:T(8,128)(2,1)}, u32[]{:S(2)}) copy-start(bf16[1024,320]{0,1:T(8,128)(2,1)} %param.10) | copy-start | bytes 1966084
  226.5 12.4 %collective-permute-start.2 = (f32[1024,128]{0,1:T(8,128)S(1)}, f32[1024,128]{0,1:T(8,128)S(1)}, u32[]{:S(2)}, u32[]{:S(2)}) collective-permute-start(f32[1024,128]{0,1:T(8,128)S(1)} %add.68), channel_id=1, source_target_pairs={{0,4},{1,5},{2,6},{3,7},{4,0},{5,1},{6,2},{7,3},{8,12},{9,13},{10,... | collective-permute-start | bytes 1572872 | tf_op jit(solution)/shard_map/ppermute | solution.py:43
  239.0 19.2 %copy-start.4 = (bf16[1024,320]{0,1:T(8,128)(2,1)S(1)}, bf16[1024,320]{0,1:T(8,128)(2,1)}, u32[]{:S(2)}) copy-start(bf16[1024,320]{0,1:T(8,128)(2,1)} %param.11) | copy-start | bytes 1966084
  239.0 18.8 %collective-permute-start.3 = (f32[1024,128]{0,1:T(8,128)S(1)}, f32[1024,128]{0,1:T(8,128)S(1)}, u32[]{:S(2)}, u32[]{:S(2)}) collective-permute-start(f32[1024,128]{0,1:T(8,128)S(1)} %add.69), channel_id=1, source_target_pairs={{0,8},{1,9},{2,10},{3,11},{4,12},{5,13},{6,14},{7,15},{8,0},{9,1},... | collective-permute-start | bytes 1572872 | tf_op jit(solution)/shard_map/ppermute | solution.py:43
  258.9 9.6 %collective-permute-start.4 = (f32[2368,64]{0,1:T(8,128)S(1)}, f32[2368,64]{0,1:T(8,128)S(1)}, u32[]{:S(2)}, u32[]{:S(2)}) collective-permute-start(f32[2368,64]{0,1:T(8,128)S(1)} %concatenate.15), channel_id=1, source_target_pairs={{0,16},{16,0},{32,48},{48,32},{64,80},{80,64},{96,112},{112,96},{1... | collective-permute-start | bytes 1818632 | tf_op jit(solution)/shard_map/ppermute | solution.py:43
  268.5 9.6 %collective-permute-start.5 = (f32[2368,64]{0,1:T(8,128)S(1)}, f32[2368,64]{0,1:T(8,128)S(1)}, u32[]{:S(2)}, u32[]{:S(2)}) collective-permute-start(f32[2368,64]{0,1:T(8,128)S(1)} %add.71), channel_id=1, source_target_pairs={{0,32},{16,48},{32,0},{48,16},{64,96},{80,112},{96,64},{112,80},{1... | collective-permute-start | bytes 1818632 | tf_op jit(solution)/shard_map/ppermute | solution.py:43
  278.2 11.1 %collective-permute-start.6 = (f32[2368,64]{0,1:T(8,128)S(1)}, f32[2368,64]{0,1:T(8,128)S(1)}, u32[]{:S(2)}, u32[]{:S(2)}) collective-permute-start(f32[2368,64]{0,1:T(8,128)S(1)} %add.72), channel_id=1, source_target_pairs={{0,64},{16,80},{32,96},{48,112},{64,0},{80,16},{96,32},{112,48},{1... | collective-permute-start | bytes 1818632 | tf_op jit(solution)/shard_map/ppermute | solution.py:43
Sparse Core Ops, SparseCore 0:
  11.8 133.3 all-gather.1
  207.5 115.5 reduce-scatter.1
where the time goes:
time: 330 us
  waiting for transfers between devices  235 us (71%)
  matrix products  68.1 us (21%)
  between operations  14.3 us (4%)
  starting transfers between devices  5.78 us (2%)
  other arithmetic  4.07 us (1%)
    all_gather x1, waiting for transfers between devices, local(): lax.all_gather(jnp.stack([tokens_in, gated_local]), 'col', axis=2, tiled=...  133 us
    ppermute x7, waiting for transfers between devices, tree_sum(): value = value + lax.ppermute(value, axis, pairs)  69.3 us
    dot_general x4, matrix products, plain_dot(): return jnp.dot(left, right, preferred_element_type=jnp.float32)  37.7 us
    reduce_scatter x1, waiting for transfers between devices, local(): lax.psum_scatter((block_part + low_part).astype(jnp.bfloat16), 'col', sca...  32.3 us
    dot_general x4, matrix products, dot_rows(): lax.dot_general(left, right, (((1,), (1,)), ((), ())), preferred_element_...  26.4 us
  transfers between devices with their start and end apart: 9, of which 9 were waited for; matrix products, arithmetic and copies ran while one was open for 3% of the time, Pallas kernels for 0%

commit v1 on v0

--- a/solution.py
+++ b/solution.py
@@ -66,7 +66,12 @@
     rank = inner_down.shape[1]
     gain_local = lax.dynamic_slice_in_dim(gate_gain, col_index * local_width, local_width, 0)
     gated_local = (gain_local[None, :] * token_grad.astype(jnp.float32)).astype(jnp.bfloat16)
-    both_full = lax.all_gather(jnp.stack([tokens_in, gated_local]), "col", axis=2, tiled=True)
+    both_full = jnp.concatenate(
+        lax.all_to_all(
+            jnp.stack([jnp.stack([tokens_in, gated_local])] * lax.axis_size("col")), "col", 0, 0
+        ),
+        axis=2,
+    )
     tokens_full, gated_full = (both_full[0], both_full[1])
     inner_cat = jnp.concatenate([inner_weight, inner_down], axis=1)
     outer_cat = jnp.concatenate([outer_weight, outer_up.T], axis=1)

time: 330 us -> 453 us (1.37)
  blocking collectives: 0 us -> 239 us
  waiting for transfers between devices: 235 us -> 100 us
  local copies, waits for them, and re-layouts: 2.66 us -> 21.8 us
    all_to_all x0 -> x1, blocking collectives: none -> 239 us  [local(): lax.all_to_all(jnp.stack([jnp.stack([tokens_in, gated_local])] * lax.axis...]
    all_gather x1 -> x0, waiting for transfers between devices: 133 us -> none  [local(): lax.all_gather(jnp.stack([tokens_in, gated_local]), 'col', axis=2, tiled=...]
    all_to_all x0 -> x1, local copies, waits for them, and re-layouts: none -> 10.3 us  [local(): lax.all_to_all(jnp.stack([jnp.stack([tokens_in, gated_local])] * lax.axis...]
    slice x0 -> x1, local copies, waits for them, and re-layouts: none -> 6.19 us  [local(): tokens_full, gated_full = (both_full[0], both_full[1])]
    reduce_scatter x1, waiting for transfers between devices: 32.3 us -> 26.6 us  [local(): lax.psum_scatter((block_part + low_part).astype(jnp.bfloat16), 'col', sca...]
  transfers between devices with their start and end apart: 9 -> 8, of which waited for: 9 -> 8; matrix products, arithmetic and copies ran while one was open for 3% -> 2% of each run, Pallas kernels for 0% -> 0%
where the time goes in v1:
time: 453 us
  blocking collectives  239 us (53%)
  waiting for transfers between devices  100 us (22%)
  matrix products  67.1 us (15%)
  local copies, waits for them, and re-layouts  21.8 us (5%)
  between operations  14.3 us (3%)
  starting transfers between devices  7.44 us (2%)
    all_to_all x1, blocking collectives, local(): lax.all_to_all(jnp.stack([jnp.stack([tokens_in, gated_local])] * lax.axis...  239 us
    ppermute x7, waiting for transfers between devices, tree_sum(): value = value + lax.ppermute(value, axis, pairs)  73.4 us
    dot_general x4, matrix products, plain_dot(): return jnp.dot(left, right, preferred_element_type=jnp.float32)  37.8 us
    reduce_scatter x1, waiting for transfers between devices, local(): lax.psum_scatter((block_part + low_part).astype(jnp.bfloat16), 'col', sca...  26.6 us
    dot_general x4, matrix products, dot_rows(): lax.dot_general(left, right, (((1,), (1,)), ((), ())), preferred_element_...  25.4 us
    all_to_all x1, local copies, waits for them, and re-layouts, local(): lax.all_to_all(jnp.stack([jnp.stack([tokens_in, gated_local])] * lax.axis...  10.3 us
  transfers between devices with their start and end apart: 8, of which 8 were waited for; matrix products, arithmetic and copies ran while one was open for 2% of the time, Pallas kernels for 0%

profile of v1, /device:TPU:1, one launch (start us, length us, event | category | flops | bytes accessed | tf_op | source)
XLA Modules:
  0.0 453.0 jit_solution(2842672419000578386)
XLA Ops:
  7.2 0.0 copy-start
  7.2 0.0 reduce-scatter.2.cloned.1.call-start
  7.2 0.8 dynamic_slice.3
  8.0 0.0 copy-start.6
  8.0 1.3 fusion.17
  9.3 0.0 copy-done.6
  9.3 1.2 pad_maximum_fusion
  10.5 2.7 stack.11
  13.2 239.4 %all_to_all.5 = bf16[16,2,1024,320]{2,3,1,0:T(8,128)(2,1)} all-to-all(bf16[16,2,1024,320]{2,3,1,0:T(8,128)(2,1)S(1)} %stack.11), channel_id=1, replica_groups=mesh['row'=8,'col'=16] {'col'}, dimensions={0} | all-to-all | bytes 41943040 | tf_op jit(solution)/shard_map/all_to_all | solution.py:70
  252.6 10.3 %copy.18 = bf16[16,2,1024,320]{2,3,0,1:T(8,128)(2,1)S(1)} copy(bf16[16,2,1024,320]{2,3,1,0:T(8,128)(2,1)} %all_to_all.5) | data formatting | bytes 41943040 | tf_op jit(solution)/shard_map/all_to_all | solution.py:70
  262.9 0.0 copy-start.8
  262.9 6.2 %fusion.26 = (bf16[1,1024,16,320]{1,3,2,0:T(8,128)(2,1)}, bf16[1,1024,16,320]{1,3,2,0:T(8,128)(2,1)S(1)}) fusion(bf16[2,1024,16,320]{1,3,2,0:T(8,128)(2,1)S(1)} %bitcast.29), kind=kLoop, calls=%fused_computation.43 | loop fusion | bytes 41943040 | tf_op jit(solution)/shard_map/slice | solution.py:75
  269.1 0.0 copy-done.8
  269.1 0.0 copy-start.3
  269.1 16.6 %fusion = f32[1024,928]{0,1:T(8,128)} fusion(bf16[1024,5120]{0,1:T(8,128)(2,1)} %bitcast.31, bf16[5120,64]{0,1:T(8,128)(2,1)S(1)} %bitcast.33, bf16[5120,864]{0,1:T(8,128)(2,1)} %param.15), kind=kOutput, calls=%fused_computation.2 | convolution fusion | flops 9749790720 | bytes 23789568 | tf_op jit(solution)/shard_map/dot_general | solution.py:24
  285.7 0.0 copy-done.3
  285.7 14.2 %fusion.4 = f32[1024,928]{0,1:T(8,128)} fusion(bf16[1024,5120]{0,1:T(8,128)(2,1)S(1)} %bitcast.30, bf16[5120,64]{0,1:T(8,128)(2,1)S(1)} %copy-done.3, bf16[5120,864]{0,1:T(8,128)(2,1)} %param.13), kind=kOutput, calls=%fused_computation.6 | convolution fusion | flops 9749790720 | bytes 23789568 | tf_op jit(solution)/shard_map/dot_general | solution.py:24
  300.0 0.0 copy-done
  300.0 0.0 copy-done.9
  300.0 4.9 %multiply_convert_fusion = (bf16[1024,864]{0,1:T(8,128)(2,1)}, f32[1024,864]{0,1:T(8,128)S(1)}) fusion(f32[864]{0:T(1024)S(1)} %copy-done.9, bf16[64,864]{1,0:T(8,128)(2,1)S(1)} %copy-done, f32[1024,928]{0,1:T(8,128)} %fusion.4), kind=kOutput, calls=%fused_computation.22 | convolution fusion | flops 123043840 | bytes 9223552 | tf_op jit(solution)/shard_map/dot_general | solution.py:24
  304.9 0.0 copy-done.5
  304.9 4.6 %fusion.14 = bf16[1024,864]{0,1:T(8,128)(2,1)S(1)} fusion(f32[1024,864]{0,1:T(8,128)S(1)} %get-tuple-element.12, f32[1024,928]{0,1:T(8,128)} %fusion, bf16[864,64]{0,1:T(8,128)(2,1)S(1)} %copy-done.5), kind=kOutput, calls=%fused_computation.18 | convolution fusion | flops 131006464 | bytes 9220096 | tf_op jit(solution)/shard_map/dot_general | solution.py:28
  309.5 0.4 fusion.29
  310.0 13.6 %fusion.28 = bf16[1024,5120]{0,1:T(8,128)(2,1)S(1)} fusion(bf16[1024,864]{0,1:T(8,128)(2,1)S(1)} %fusion.14, bf16[5120,864]{0,1:T(8,128)(2,1)} %param.13), kind=kOutput, calls=%fused_computation.45 | convolution fusion | flops 9059696640 | bytes 21102592 | tf_op jit(solution)/shard_map/dot_general | solution.py:28
  323.5 6.8 %add_convert_fusion = bf16[1024,5120]{0,1:T(8,128)(2,1)} fusion(bf16[5120,64]{0,1:T(8,128)(2,1)} %param.16, bf16[1024,5120]{0,1:T(8,128)(2,1)S(1)} %fusion.28, f32[1024,64]{0,1:T(8,128)S(1)} %fusion.29), kind=kOutput, calls=%fused_computation.1 | convolution fusion | flops 686882816 | bytes 21889024 | tf_op jit(solution)/shard_map/dot_general | solution.py:28
  330.3 0.0 reduce-scatter.2.cloned.1.call-update
  330.3 0.0 copy-start.1
  330.3 2.0 fusion.30
  332.4 1.6 collective-permute-start
  334.1 1.5 collective-permute-done
  335.6 0.1 fusion.25
  335.7 0.3 collective-permute-start.1
  336.0 14.4 %collective-permute-done.1 = f32[1024,128]{0,1:T(8,128)S(1)} collective-permute-done((f32[1024,128]{0,1:T(8,128)S(1)}, f32[1024,128]{0,1:T(8,128)S(1)}, u32[]{:S(2)}, u32[]{:S(2)}) %collective-permute-start.1) | collective-permute-done | bytes 524320 | tf_op jit(solution)/shard_map/ppermute | solution.py:43
  350.4 0.1 add.68
  350.5 0.0 copy-start.2
  350.5 0.1 collective-permute-start.2
  350.6 12.2 %collective-permute-done.2 = f32[1024,128]{0,1:T(8,128)S(1)} collective-permute-done((f32[1024,128]{0,1:T(8,128)S(1)}, f32[1024,128]{0,1:T(8,128)S(1)}, u32[]{:S(2)}, u32[]{:S(2)}) %collective-permute-start.2) | collective-permute-done | bytes 524320 | tf_op jit(solution)/shard_map/ppermute | solution.py:43
  362.8 0.1 add.69
  362.9 0.0 copy-start.4
  362.9 0.0 copy-start.7
  362.9 1.3 collective-permute-start.3
  364.1 0.0 copy-done.1
  364.1 1.6 fusion.21
  365.7 1.6 fusion.22
  367.4 11.6 %collective-permute-done.3 = f32[1024,128]{0,1:T(8,128)S(1)} collective-permute-done((f32[1024,128]{0,1:T(8,128)S(1)}, f32[1024,128]{0,1:T(8,128)S(1)}, u32[]{:S(2)}, u32[]{:S(2)}) %collective-permute-start.3) | collective-permute-done | bytes 524320 | tf_op jit(solution)/shard_map/ppermute | solution.py:43
  378.9 0.1 add_convert_fusion.1
  379.0 0.0 copy-done.2
  379.0 0.3 convolution_bitcast_fusion
  379.4 0.0 copy-done.4
  379.4 0.0 copy-done.7
  379.4 0.4 fusion.16
  379.8 0.2 concatenate.15
  380.0 0.2 collective-permute-start.4
  380.2 12.0 %collective-permute-done.4 = f32[2368,64]{0,1:T(8,128)S(1)} collective-permute-done((f32[2368,64]{0,1:T(8,128)S(1)}, f32[2368,64]{0,1:T(8,128)S(1)}, u32[]{:S(2)}, u32[]{:S(2)}) %collective-permute-start.4) | collective-permute-done | bytes 606240 | tf_op jit(solution)/shard_map/ppermute | solution.py:43
  392.1 0.1 add.71
  392.2 1.2 collective-permute-start.5
  393.5 8.3 %collective-permute-done.5 = f32[2368,64]{0,1:T(8,128)S(1)} collective-permute-done((f32[2368,64]{0,1:T(8,128)S(1)}, f32[2368,64]{0,1:T(8,128)S(1)}, u32[]{:S(2)}, u32[]{:S(2)}) %collective-permute-start.5) | collective-permute-done | bytes 606240 | tf_op jit(solution)/shard_map/ppermute | solution.py:43
  401.8 0.1 add.72
  401.8 2.7 collective-permute-start.6
  404.5 13.4 %collective-permute-done.6 = f32[2368,64]{0,1:T(8,128)S(1)} collective-permute-done((f32[2368,64]{0,1:T(8,128)S(1)}, f32[2368,64]{0,1:T(8,128)S(1)}, u32[]{:S(2)}, u32[]{:S(2)}) %collective-permute-start.6) | collective-permute-done | bytes 606240 | tf_op jit(solution)/shard_map/ppermute | solution.py:43
  417.9 0.1 add_multiply_fusion
  418.0 0.7 slice_bitcast_fusion.1
  418.8 0.8 fusion.27
  419.6 26.6 %reduce-scatter.2.cloned.1.call-done = bf16[1024,320]{0,1:T(8,128)(2,1)} async-done(((bf16[1024,5120]{0,1:T(8,128)(2,1)}), bf16[1024,320]{0,1:T(8,128)(2,1)}) %reduce-scatter.2.cloned.1.call-update) | async-done | bytes 655376 | tf_op jit(solution)/shard_map/reduce_scatter | solution.py:91
  (3 shorter events, 0.0 us)
Async XLA Ops:
  7.2 292.8 %copy-start = (bf16[64,864]{1,0:T(8,128)(2,1)S(1)}, bf16[64,864]{1,0:T(8,128)(2,1)}, u32[]{:S(2)}) copy-start(bf16[64,864]{1,0:T(8,128)(2,1)} %param.17) | copy-start | bytes 331780
  7.2 439.0 %reduce-scatter.2.cloned.1.call-start = ((), (), s32[]{:S(2)}) async-start(), calls=%async_computation.2 | async-start | bytes 11141120 | tf_op jit(solution)/shard_map/reduce_scatter | solution.py:91
  8.0 1.3 copy-start.6
  262.9 6.2 %copy-start.8 = (bf16[64,5120]{1,0:T(8,128)(2,1)S(1)}, bf16[64,5120]{1,0:T(8,128)(2,1)}, u32[]{:S(2)}) copy-start(bf16[64,5120]{1,0:T(8,128)(2,1)} %param.19) | copy-start | bytes 1966084
  269.1 16.6 %copy-start.3 = (bf16[5120,64]{0,1:T(8,128)(2,1)S(1)}, bf16[5120,64]{0,1:T(8,128)(2,1)}, u32[]{:S(2)}) copy-start(bf16[5120,64]{0,1:T(8,128)(2,1)} %param.16) | copy-start | bytes 1966084
  285.7 14.2 %copy-start.9 = (f32[864]{0:T(1024)S(1)}, f32[864]{0:T(1024)}, u32[]{:S(2)}) copy-start(f32[864]{0:T(1024)} %param.14) | copy-start | bytes 10372
  300.0 4.9 %copy-start.5 = (bf16[864,64]{0,1:T(8,128)(2,1)S(1)}, bf16[864,64]{0,1:T(8,128)(2,1)}, u32[]{:S(2)}) copy-start(bf16[864,64]{0,1:T(8,128)(2,1)} %param.18) | copy-start | bytes 331780
  330.3 33.8 %copy-start.1 = (bf16[1024,864]{0,1:T(8,128)(2,1)S(1)}, bf16[1024,864]{0,1:T(8,128)(2,1)}, u32[]{:S(2)}) copy-start(bf16[1024,864]{0,1:T(8,128)(2,1)} %get-tuple-element.11) | copy-start | bytes 5308420
  332.4 3.2 collective-permute-start
  335.7 14.7 %collective-permute-start.1 = (f32[1024,128]{0,1:T(8,128)S(1)}, f32[1024,128]{0,1:T(8,128)S(1)}, u32[]{:S(2)}, u32[]{:S(2)}) collective-permute-start(f32[1024,128]{0,1:T(8,128)S(1)} %fusion.25), channel_id=1, source_target_pairs={{0,2},{1,3},{2,0},{3,1},{4,6},{5,7},{6,4},{7,5},{8,10},{9,11},{10,... | collective-permute-start | bytes 1572872 | tf_op jit(solution)/shard_map/ppermute | solution.py:43
  350.5 28.5 %copy-start.2 = (bf16[1024,320]{0,1:T(8,128)(2,1)S(1)}, bf16[1024,320]{0,1:T(8,128)(2,1)}, u32[]{:S(2)}) copy-start(bf16[1024,320]{0,1:T(8,128)(2,1)} %param.10) | copy-start | bytes 1966084
  350.5 12.3 %collective-permute-start.2 = (f32[1024,128]{0,1:T(8,128)S(1)}, f32[1024,128]{0,1:T(8,128)S(1)}, u32[]{:S(2)}, u32[]{:S(2)}) collective-permute-start(f32[1024,128]{0,1:T(8,128)S(1)} %add.68), channel_id=1, source_target_pairs={{0,4},{1,5},{2,6},{3,7},{4,0},{5,1},{6,2},{7,3},{8,12},{9,13},{10,... | collective-permute-start | bytes 1572872 | tf_op jit(solution)/shard_map/ppermute | solution.py:43
  362.9 16.5 %copy-start.4 = (bf16[1024,320]{0,1:T(8,128)(2,1)S(1)}, bf16[1024,320]{0,1:T(8,128)(2,1)}, u32[]{:S(2)}) copy-start(bf16[1024,320]{0,1:T(8,128)(2,1)} %param.11) | copy-start | bytes 1966084
  362.9 16.5 %copy-start.7 = (f32[320]{0:T(512)S(1)}, f32[320]{0:T(512)}, u32[]{:S(2)}) copy-start(f32[320]{0:T(512)} %copy-done.6) | copy-start | bytes 3844
  362.9 16.0 %collective-permute-start.3 = (f32[1024,128]{0,1:T(8,128)S(1)}, f32[1024,128]{0,1:T(8,128)S(1)}, u32[]{:S(2)}, u32[]{:S(2)}) collective-permute-start(f32[1024,128]{0,1:T(8,128)S(1)} %add.69), channel_id=1, source_target_pairs={{0,8},{1,9},{2,10},{3,11},{4,12},{5,13},{6,14},{7,15},{8,0},{9,1},... | collective-permute-start | bytes 1572872 | tf_op jit(solution)/shard_map/ppermute | solution.py:43
  380.0 12.1 %collective-permute-start.4 = (f32[2368,64]{0,1:T(8,128)S(1)}, f32[2368,64]{0,1:T(8,128)S(1)}, u32[]{:S(2)}, u32[]{:S(2)}) collective-permute-start(f32[2368,64]{0,1:T(8,128)S(1)} %concatenate.15), channel_id=1, source_target_pairs={{0,16},{16,0},{32,48},{48,32},{64,80},{80,64},{96,112},{112,96},{1... | collective-permute-start | bytes 1818632 | tf_op jit(solution)/shard_map/ppermute | solution.py:43
  392.2 9.6 %collective-permute-start.5 = (f32[2368,64]{0,1:T(8,128)S(1)}, f32[2368,64]{0,1:T(8,128)S(1)}, u32[]{:S(2)}, u32[]{:S(2)}) collective-permute-start(f32[2368,64]{0,1:T(8,128)S(1)} %add.71), channel_id=1, source_target_pairs={{0,32},{16,48},{32,0},{48,16},{64,96},{80,112},{96,64},{112,80},{1... | collective-permute-start | bytes 1818632 | tf_op jit(solution)/shard_map/ppermute | solution.py:43
  401.8 16.1 %collective-permute-start.6 = (f32[2368,64]{0,1:T(8,128)S(1)}, f32[2368,64]{0,1:T(8,128)S(1)}, u32[]{:S(2)}, u32[]{:S(2)}) collective-permute-start(f32[2368,64]{0,1:T(8,128)S(1)} %add.72), channel_id=1, source_target_pairs={{0,64},{16,80},{32,96},{48,112},{64,0},{80,16},{96,32},{112,48},{1... | collective-permute-start | bytes 1818632 | tf_op jit(solution)/shard_map/ppermute | solution.py:43
Sparse Core Ops, SparseCore 0:
  330.5 115.6 reduce-scatter.1
